TPU v7x, 32 devices: a whole 2x2x4 slice. The times are simulated.
32 devices in a mesh: rows: 8 (over z, y), cols: 4 (over x, core).
Axes of the slice: x: 2, y: 2, z: 4, core: 2. Of those that a mesh axis runs over, the one named last changes fastest.
Arguments:
- coefficients: float32 [4, 1024, 4, 256], P(None, 'rows'), may hold values from -0.03 to 0.09
- support: int32 [4, 1024, 4], P(None, 'rows'), may hold values from 0 to 11, all different within a row
- primal: float32 [12, 256, 256], P('cols'), may hold values from -0.5 to 9, as said below
- dual_inverse: float32 [12, 256, 256], P('cols'), may hold values from -0.5 to 9, as said below
- block_sizes: int32 [12], P('cols'), may hold values from 64 to 256, as said below
- damping: float32 [4, 1024], P(None, 'rows'), may hold values from 0.5 to 2
- right_sides: float32 [4, 32, 1024], P(None, 'cols', 'rows'), may hold values from -6 to 6
Outputs:
- updated: float32 [4, 1024, 4096], P(None, 'rows', 'cols')
- panel_factor: float32 [4, 1024, 128], P(None, 'rows')
- solved: float32 [4, 32, 1024], P(None, 'cols', 'rows')
Inputs may be any that keep to these rules, and one draw needn't show every extreme that they name: `primal`: each block is symmetric positive definite. `dual_inverse`: each block is symmetric positive definite. `block_sizes`: some block has order 256.
All inputs are finite; a program needn't handle non-finite values.
Results may differ from a plain program's by a relative error of at most 0.00015.
Values sent between devices are 32-bit elements; how exact they have to be, the bound alone decides.
A program may use at most 192 MiB of HBM per device.

v0:
```python
import jax
import jax.numpy as jnp
from jax import lax
from jax.sharding import PartitionSpec as P

BS = 256
K = 4
TILE = 128
TPR = 4
highest = lax.Precision.HIGHEST


def broadcast(block, axis, holder):
    block = jnp.where(lax.axis_index(axis) == holder, block, jnp.zeros_like(block))
    return lax.psum(block, axis)


def densify(values, labels, owned_blocks):
    chosen = (labels[..., None] == owned_blocks).astype(jnp.float32)
    return jnp.einsum("tnkq,tnkd->tnqd", chosen, values, precision=highest)


def local(coefficients, support, primal, dual_inverse, block_sizes, damping, right_sides):
    col_index = lax.axis_index("cols")
    row_index = lax.axis_index("rows")
    rows_total = lax.axis_size("rows")
    cols_total = lax.axis_size("cols")
    count_all = TPR * TILE * rows_total
    col_width = count_all // cols_total
    positions = jnp.arange(BS, dtype=jnp.int32)
    active = (positions[None, :] < block_sizes[:, None]).astype(jnp.float32)
    weights = primal * dual_inverse * active[:, :, None] * active[:, None, :]
    every_weight = lax.all_gather(weights, "cols", axis=0, tiled=True)
    all_blocks = jnp.arange(every_weight.shape[0], dtype=jnp.int32)
    own_dense = densify(coefficients, support, all_blocks)
    weighted = jnp.einsum("taqd,qde->taqe", own_dense, every_weight, precision=highest)
    every_coef, every_support = (
        lax.all_gather(coefficients, "rows", axis=1, tiled=True),
        lax.all_gather(support, "rows", axis=1, tiled=True),
    )
    flat_coef = every_coef.reshape(count_all, K, BS)
    flat_support = every_support.reshape(count_all, K)
    column_coef = lax.dynamic_slice_in_dim(flat_coef, col_index * col_width, col_width, 0)
    column_support = lax.dynamic_slice_in_dim(flat_support, col_index * col_width, col_width, 0)
    column_dense = densify(column_coef[None], column_support[None], all_blocks)[0]
    schur_rows = jnp.einsum("taqe,nqe->tan", weighted, column_dense, precision=highest)
    row_global = (jnp.arange(TPR)[:, None] * rows_total + row_index) * TILE + jnp.arange(TILE)[
        None, :
    ]
    col_global = col_index * col_width + jnp.arange(col_width)
    on_diagonal = row_global[:, :, None] == col_global[None, None, :]
    schur_rows = schur_rows + jnp.where(on_diagonal, damping[:, :, None], 0.0)
    corner = broadcast(schur_rows[0, :, :TILE], ("rows", "cols"), 0)
    top_sides = broadcast(right_sides[0], "rows", 0)
    factor = jnp.linalg.cholesky(corner)
    inverse = jax.scipy.linalg.solve_triangular(
        factor, jnp.eye(TILE, dtype=jnp.float32), lower=True
    )
    candidate = jnp.einsum("tak,jk->taj", schur_rows[:, :, :TILE], inverse, precision=highest)
    panel_factor = broadcast(candidate, "cols", 0)
    every_row = lax.all_gather(panel_factor, "rows", axis=1, tiled=True).reshape(count_all, TILE)
    column_panel = lax.dynamic_slice_in_dim(every_row, col_index * col_width, col_width, 0)
    outer_term = jnp.einsum("tak,mk->tam", panel_factor, column_panel, precision=highest)
    row_later = row_global[:, 0] >= TILE
    col_later = col_global >= TILE
    updated = schur_rows - jnp.where(
        row_later[:, None, None] & col_later[None, None, :], outer_term, 0.0
    )
    leading = jnp.dot(top_sides, inverse.T, precision=highest, preferred_element_type=jnp.float32)
    remainder = right_sides - jnp.einsum("sk,tak->tsa", leading, panel_factor, precision=highest)
    solved = jnp.where(row_later[:, None, None], remainder, leading[None, :, :])
    return (updated, panel_factor, solved)


def solution(mesh):
    in_specs = (
        P(None, "rows", None, None),
        P(None, "rows", None),
        P("cols", None, None),
        P("cols", None, None),
        P("cols"),
        P(None, "rows"),
        P(None, "cols", "rows"),
    )
    out_specs = (P(None, "rows", "cols"), P(None, "rows", None), P(None, "cols", "rows"))
    return jax.shard_map(local, mesh=mesh, in_specs=in_specs, out_specs=out_specs, check_vma=False)
```

profile of v0, /device:TPU:0, one launch (start us, length us, event | category | flops | bytes accessed | tf_op | source)
XLA Modules:
  0.0 572.3 jit_solution(2047306640802316005)
XLA Ops:
  7.2 0.0 all-gather.4.cloned.1.call-start
  7.2 0.7 fusion.28
  7.9 0.0 copy-start.3
  7.9 2.4 multiply_multiply_fusion
  10.4 0.0 all-gather.4.cloned.1.call-update
  10.4 0.0 all-gather.6.cloned.1.call-start
  10.4 0.7 all-gather.6.cloned.1.call-update
  11.1 0.0 all-reduce.3.cloned.1.call-start
  11.2 0.0 copy-done.3
  11.2 0.1 copy.25
  11.4 27.8 %all_gather.13 = s32[4,1024,4]{1,2,0:T(4,128)S(1)} all-gather(s32[4,128,4]{1,2,0:T(4,128)S(1)} %copy-done.3), channel_id=1, replica_groups=mesh['rows'=8,'cols'=4] {'rows'}, dimensions={1}, use_global_device_ids=true | all-gather | bytes 73728 | tf_op jit(solution)/shard_map/all_gather | solution.py:39
  39.2 0.2 copy.28
  39.4 0.1 copy.31
  39.5 0.0 copy-done.1
  39.5 7.4 %fusion.16 = f32[4,128,12,256]{3,2,1,0:T(8,128)} fusion(f32[4,128,4,256]{3,2,1,0:T(4,128)S(1)} %copy-done.1, s32[4,128,4]{2,1,0:T(8,128)S(1)} %copy.25), kind=kOutput, calls=%fused_computation.18 | convolution fusion | flops 75522048 | bytes 8396800 | tf_op jit(solution)/shard_map/tnkq,tnkd->tnqd/dot_general | solution.py:20
  46.9 18.5 %fusion.4 = f32[12,256,4,128]{3,1,0,2:T(8,128)} fusion(f32[4,128,12,256]{3,2,1,0:T(8,128)} %fusion.16, f32[12,256,256]{2,1,0:T(8,128)} %all-gather.4.cloned.1.call-done), kind=kOutput, calls=%fused_computation.4 | convolution fusion | flops 4831838208 | bytes 15728640 | tf_op jit(solution)/shard_map/taqd,qde->taqe/dot_general | solution.py:36
  65.4 205.8 %all-gather.6.cloned.1.call-done = f32[4,1024,4,256]{3,2,1,0:T(4,128)} async-done(((f32[4,128,4,256]{3,2,1,0:T(4,128)}), f32[4,1024,4,256]{3,2,1,0:T(4,128)}) %all-gather.6.cloned.1.call-update) | async-done | bytes 16777232 | tf_op jit(solution)/shard_map/all_gather | solution.py:38
  271.3 25.9 %fusion.6 = f32[1024,12,256]{2,1,0:T(8,128)S(1)} fusion(f32[4096,4,256]{2,1,0:T(4,128)} %bitcast.53, s32[]{:T(128)S(6)} %select_n.51, s32[1024,4]{1,0:T(8,128)S(1)} %copy.28), kind=kOutput, calls=%fused_computation.6 | convolution fusion | flops 151044096 | bytes 16793604 | tf_op jit(solution)/shard_map/tnkq,tnkd->tnqd/dot_general | solution.py:20
  297.1 0.0 copy-done
  297.2 0.0 copy-done.5
  297.2 0.0 copy-start.4
  297.2 30.9 %bitcast_add_fusion = f32[4,128,1024]{1,2,0:T(8,128)S(1)} fusion(f32[1024,12,256]{2,1,0:T(8,128)S(1)} %fusion.6, f32[12,256,4,128]{3,1,0,2:T(8,128)S(1)} %copy-done, f32[4,128]{1,0:T(4,128)S(1)} %copy-done.5, s32[4,128]{1,0:T(4,128)S(1)} %copy.31, s32[1024]{0:T(1024)S(1)} %iota_add_fusion.1), kind=kOutput, calls=%fused_computation.9 | convolution fusion | flops 19328925696 | bytes 20979712 | tf_op jit(solution)/shard_map/taqe,nqe->tan/dot_general | solution.py:46
  328.1 0.6 fusion.22
  328.8 0.0 all-reduce.3.cloned.1.call-update
  328.8 0.0 all-reduce.5.cloned.1.call-start
  328.8 117.6 %all-reduce.3.cloned.1.call-done = f32[128,128]{0,1:T(8,128)} async-done(((f32[128,128]{0,1:T(8,128)}), f32[128,128]{0,1:T(8,128)}) %all-reduce.3.cloned.1.call-update) | async-done | bytes 65552 | tf_op jit(solution)/shard_map/psum | solution.py:15
  446.4 0.9 copy.33
  447.4 0.9 fusion.26
  448.2 11.7 %cholesky.16 = f32[128,128]{1,0:T(8,128)S(1)} custom-call(f32[128,128]{1,0:T(8,128)S(1)} %fusion.26), custom_call_target="Cholesky" | custom-call | tf_op jit(solution)/shard_map/jit(cholesky)/cholesky | solution.py:55
  460.0 0.6 compare_reduce_fusion
  460.6 0.7 fusion.21
  461.3 9.8 %custom-call.7 = f32[1,128,128]{1,2,0:T(8,128)S(1)} custom-call(f32[1,128,128]{2,1,0:T(8,128)S(1)} %fusion.21), custom_call_target="InvertDiagBlocksLowerTriangular" | custom-call | tf_op jit(solution)/shard_map/jit(_solve_triangular)/triangular_solve | solution.py:56
  471.1 0.2 fusion.24
  471.4 1.3 convolution_select_fusion
  472.7 0.0 all-reduce.5.cloned.1.call-update
  472.7 0.0 all-gather.8.cloned.1.call-start
  472.7 33.6 %all-reduce.5.cloned.1.call-done = f32[4,128,128]{2,1,0:T(8,128)} async-done(((f32[4,128,128]{2,1,0:T(8,128)}), f32[4,128,128]{2,1,0:T(8,128)}) %all-reduce.5.cloned.1.call-update) | async-done | bytes 262160 | tf_op jit(solution)/shard_map/psum | solution.py:15
  506.4 0.0 all-gather.8.cloned.1.call-update
  506.4 0.0 copy-done.4
  506.4 21.6 %psum.23 = f32[8,128]{1,0:T(8,128)S(1)} all-reduce(f32[8,128]{1,0:T(8,128)S(1)} %select_bitcast_fusion), channel_id=1, replica_groups=mesh['rows'=8,'cols'=4] {'rows'}, use_global_device_ids=true, to_apply=%region_4.5 | all-reduce | flops 1024 | bytes 8192 | tf_op jit(solution)/shard_map/psum | solution.py:15
  528.0 0.1 broadcast_and_fusion
  528.1 0.2 fusion.31
  528.3 1.9 fusion.14
  530.2 27.4 %all-gather.8.cloned.1.call-done = f32[4,1024,128]{2,1,0:T(8,128)} async-done(((f32[4,128,128]{2,1,0:T(8,128)}), f32[4,1024,128]{2,1,0:T(8,128)}) %all-gather.8.cloned.1.call-update) | async-done | bytes 2097168 | tf_op jit(solution)/shard_map/all_gather | solution.py:61
  557.6 4.1 select_subtract_fusion
  561.8 2.9 copy.36
  564.7 0.0 copy-done.2
  564.7 0.7 copy.54
  (13 shorter events, 0.1 us)
Async XLA Ops:
  7.2 39.7 %all-gather.4.cloned.1.call-start = ((), (), s32[]{:S(2)}) async-start(), calls=%async_computation | async-start | bytes 3932160 | tf_op jit(solution)/shard_map/all_gather | solution.py:33
  7.9 3.3 copy-start.3
  10.4 29.1 %copy-start.1 = (f32[4,128,4,256]{3,2,1,0:T(4,128)S(1)}, f32[4,128,4,256]{3,2,1,0:T(4,128)}, u32[]{:S(2)}) copy-start(f32[4,128,4,256]{3,2,1,0:T(4,128)} %param.7) | copy-start | bytes 6291460
  10.4 260.9 %all-gather.6.cloned.1.call-start = ((), (), s32[]{:S(2)}) async-start(), calls=%async_computation.1 | async-start | bytes 18874368 | tf_op jit(solution)/shard_map/all_gather | solution.py:38
  11.1 435.3 %all-reduce.3.cloned.1.call-start = ((), (), s32[]{:S(2)}) async-start(), calls=%async_computation.2 | async-start | bytes 131072 | tf_op jit(solution)/shard_map/psum | solution.py:15
  271.3 25.9 %copy-start = (f32[12,256,4,128]{3,1,0,2:T(8,128)S(1)}, f32[12,256,4,128]{3,1,0,2:T(8,128)}, u32[]{:S(2)}) copy-start(f32[12,256,4,128]{3,1,0,2:T(8,128)} %fusion.4) | copy-start | bytes 18874372
  271.3 25.9 %copy-start.5 = (f32[4,128]{1,0:T(4,128)S(1)}, f32[4,128]{1,0:T(4,128)}, u32[]{:S(2)}) copy-start(f32[4,128]{1,0:T(4,128)} %param.12) | copy-start | bytes 6148
  297.2 209.2 %copy-start.4 = (f32[4,8,128]{2,1,0:T(8,128)S(1)}, f32[4,8,128]{2,1,0:T(8,128)}, u32[]{:S(2)}) copy-start(f32[4,8,128]{2,1,0:T(8,128)} %param.13) | copy-start | bytes 49156
  328.8 177.6 %all-reduce.5.cloned.1.call-start = ((), (), s32[]{:S(2)}) async-start(), calls=%async_computation.3 | async-start | bytes 524288 | tf_op jit(solution)/shard_map/psum | solution.py:15
  472.7 85.0 %all-gather.8.cloned.1.call-start = ((), (), s32[]{:S(2)}) async-start(), calls=%async_computation.4 | async-start | bytes 2359296 | tf_op jit(solution)/shard_map/all_gather | solution.py:61
  561.8 2.9 copy-start.2
Sparse Core Ops, SparseCore 0:
  10.5 31.2 all-gather.3
  44.0 227.2 all-gather.5
  328.9 117.4 all-reduce.2
  472.8 33.5 all-reduce.4
  508.4 49.1 all-gather.7
where the time goes:
time: 580 us; the launch traced here: 572 us
  waiting for transfers between devices  385 us (66%)
  matrix products  90.5 us (16%)
  blocking collectives  49.4 us (9%)
  other arithmetic  27.6 us (5%)
  between operations  14.3 us (2%)
    all_gather x1, waiting for transfers between devices, local(): lax.all_gather(coefficients, 'rows', axis=1, tiled=True)  206 us
    psum x2, waiting for transfers between devices, broadcast(): return lax.psum(block, axis)  151 us
    dot_general x2, matrix products, densify(): return jnp.einsum('tnkq,tnkd->tnqd', chosen, values, precision=highest)  33.3 us
    dot_general x1, matrix products, local(): jnp.einsum('taqe,nqe->tan', weighted, column_dense, precision=highest)  30.9 us
    all_gather x1, blocking collectives, local(): lax.all_gather(support, 'rows', axis=1, tiled=True)  27.8 us
    all_gather x1, waiting for transfers between devices, local(): lax.all_gather(panel_factor, 'rows', axis=1, tiled=True)  27.4 us
    psum x1, blocking collectives, broadcast(): return lax.psum(block, axis)  21.6 us
    dot_general x1, matrix products, local(): jnp.einsum('taqd,qde->taqe', own_dense, every_weight, precision=highest)  18.5 us
  transfers between devices with their start and end apart: 5, of which 4 were waited for; matrix products, arithmetic and copies ran while one was open for 5% of the time, Pallas kernels for 0%

commit v1 on v0

--- a/solution.py
+++ b/solution.py
@@ -12,7 +12,7 @@
 
 def broadcast(block, axis, holder):
     block = jnp.where(lax.axis_index(axis) == holder, block, jnp.zeros_like(block))
-    return lax.psum(block, axis)
+    return jnp.sum(lax.all_gather(block, axis), axis=0)
 
 
 def densify(values, labels, owned_blocks):

time: 580 us -> 489 us (0.84); the launches traced: 572 us -> 489 us
  waiting for transfers between devices: 385 us -> 293 us
  blocking collectives: 49.4 us -> 58.6 us
    psum x2 -> x0, waiting for transfers between devices: 151 us -> none  [broadcast(): return lax.psum(block, axis)]
    all_gather x0 -> x2, waiting for transfers between devices: none -> 69.9 us  [broadcast(): return jnp.sum(lax.all_gather(block, axis), axis=0)]
    all_gather x0 -> x1, blocking collectives: none -> 30.8 us  [broadcast(): return jnp.sum(lax.all_gather(block, axis), axis=0)]
    psum x1 -> x0, blocking collectives: 21.6 us -> none  [broadcast(): return lax.psum(block, axis)]
    dot_general x1, matrix products: 30.9 us -> 45.9 us  [local(): jnp.einsum('taqe,nqe->tan', weighted, column_dense, precision=highest)]
    dot_general x2, matrix products: 33.3 us -> 19.5 us  [densify(): return jnp.einsum('tnkq,tnkd->tnqd', chosen, values, precision=highest)]
    all_gather x1, waiting for transfers between devices: 27.4 us -> 16.7 us  [local(): lax.all_gather(panel_factor, 'rows', axis=1, tiled=True)]
  transfers between devices with their start and end apart: 5 -> 5, of which waited for: 4 -> 4; matrix products, arithmetic and copies ran while one was open for 5% -> 6% of each run, Pallas kernels for 0% -> 0%
where the time goes in v1:
time: 489 us
  waiting for transfers between devices  293 us (60%)
  matrix products  91.7 us (19%)
  blocking collectives  58.6 us (12%)
  other arithmetic  30.5 us (6%)
  between operations  13.9 us (3%)
    all_gather x1, waiting for transfers between devices, local(): lax.all_gather(coefficients, 'rows', axis=1, tiled=True)  206 us
    all_gather x2, waiting for transfers between devices, broadcast(): return jnp.sum(lax.all_gather(block, axis), axis=0)  69.9 us
    dot_general x1, matrix products, local(): jnp.einsum('taqe,nqe->tan', weighted, column_dense, precision=highest)  45.9 us
    all_gather x1, blocking collectives, broadcast(): return jnp.sum(lax.all_gather(block, axis), axis=0)  30.8 us
    all_gather x1, blocking collectives, local(): lax.all_gather(support, 'rows', axis=1, tiled=True)  27.8 us
    dot_general x2, matrix products, densify(): return jnp.einsum('tnkq,tnkd->tnqd', chosen, values, precision=highest)  19.5 us
    dot_general x1, matrix products, local(): jnp.einsum('taqd,qde->taqe', own_dense, every_weight, precision=highest)  18.5 us
    all_gather x1, waiting for transfers between devices, local(): lax.all_gather(panel_factor, 'rows', axis=1, tiled=True)  16.7 us
  transfers between devices with their start and end apart: 5, of which 4 were waited for; matrix products, arithmetic and copies ran while one was open for 6% of the time, Pallas kernels for 0%

profile of v1, /device:TPU:0, one launch (start us, length us, event | category | flops | bytes accessed | tf_op | source)
XLA Modules:
  0.0 488.9 jit_solution(17123197717625786480)
XLA Ops:
  7.2 0.0 all-gather.7.cloned.1.call-start
  7.2 0.7 fusion.27
  7.9 0.0 copy-start.2
  7.9 2.4 multiply_multiply_fusion
  10.4 0.0 copy-start.1
  10.4 0.0 all-gather.7.cloned.1.call-update
  10.4 0.0 all-gather.9.cloned.1.call-start
  10.4 0.7 all-gather.9.cloned.1.call-update
  11.1 0.0 all-gather.11.cloned.1.call-start
  11.2 0.0 copy-done.2
  11.2 0.1 copy.17
  11.4 27.8 %all_gather.27 = s32[4,1024,4]{1,2,0:T(4,128)S(1)} all-gather(s32[4,128,4]{1,2,0:T(4,128)S(1)} %copy-done.2), channel_id=1, replica_groups=mesh['rows'=8,'cols'=4] {'rows'}, dimensions={1}, use_global_device_ids=true | all-gather | bytes 73728 | tf_op jit(solution)/shard_map/all_gather | solution.py:39
  39.2 0.2 copy.20
  39.4 0.1 copy.23
  39.5 0.0 copy-done.1
  39.5 7.4 %fusion.16 = f32[4,128,12,256]{3,2,1,0:T(8,128)} fusion(f32[4,128,4,256]{3,2,1,0:T(4,128)S(1)} %copy-done.1, s32[4,128,4]{2,1,0:T(8,128)S(1)} %copy.17), kind=kOutput, calls=%fused_computation.18 | convolution fusion | flops 75522048 | bytes 8396800 | tf_op jit(solution)/shard_map/tnkq,tnkd->tnqd/dot_general | solution.py:20
  46.9 0.0 all-gather.7.cloned.1.call-done
  46.9 18.5 %fusion.4 = f32[12,256,4,128]{3,1,0,2:T(8,128)} fusion(f32[4,128,12,256]{3,2,1,0:T(8,128)} %fusion.16, f32[12,256,256]{2,1,0:T(8,128)} %all-gather.7.cloned.1.call-done), kind=kOutput, calls=%fused_computation.4 | convolution fusion | flops 4831838208 | bytes 15728640 | tf_op jit(solution)/shard_map/taqd,qde->taqe/dot_general | solution.py:36
  65.4 205.8 %all-gather.9.cloned.1.call-done = f32[4,1024,4,256]{3,2,1,0:T(4,128)} async-done(((f32[4,128,4,256]{3,2,1,0:T(4,128)}), f32[4,1024,4,256]{3,2,1,0:T(4,128)}) %all-gather.9.cloned.1.call-update) | async-done | bytes 16777232 | tf_op jit(solution)/shard_map/all_gather | solution.py:38
  271.3 12.0 %fusion.6 = f32[1024,12,256]{2,1,0:T(8,128)S(1)} fusion(f32[4096,4,256]{2,1,0:T(4,128)} %bitcast.52, s32[]{:T(128)S(6)} %select_n.47, s32[1024,4]{1,0:T(8,128)S(1)} %copy.20), kind=kOutput, calls=%fused_computation.6 | convolution fusion | flops 151044096 | bytes 16793604 | tf_op jit(solution)/shard_map/tnkq,tnkd->tnqd/dot_general | solution.py:20
  283.3 0.0 copy-done
  283.3 0.0 copy-done.4
  283.3 45.9 %bitcast_add_fusion = f32[4,128,1024]{2,1,0:T(8,128)S(1)} fusion(f32[1024,12,256]{2,1,0:T(8,128)S(1)} %fusion.6, f32[12,256,4,128]{3,1,0,2:T(8,128)S(1)} %copy-done, f32[4,128]{1,0:T(4,128)S(1)} %copy-done.4, s32[1024]{0:T(1024)S(1)} %iota_add_fusion.1, s32[4,128]{1,0:T(4,128)S(1)} %copy.23), kind=kOutput, calls=%fused_computation.9 | convolution fusion | flops 19328925696 | bytes 20979712 | tf_op jit(solution)/shard_map/taqe,nqe->tan/dot_general | solution.py:46
  329.3 0.6 slice_select_fusion
  329.9 0.0 all-gather.11.cloned.1.call-update
  330.0 0.3 all-gather.15.cloned.1.call-start
  330.2 0.0 copy-start.3
  330.3 54.2 %all-gather.11.cloned.1.call-done = f32[32,128,128]{2,1,0:T(8,128)} async-done(((f32[1,128,128]{2,1,0:T(8,128)}), f32[32,128,128]{2,1,0:T(8,128)}) %all-gather.11.cloned.1.call-update) | async-done | bytes 2097168 | tf_op jit(solution)/shard_map/all_gather | solution.py:15
  384.5 1.7 reduce_sum.27
  386.2 0.1 copy.24
  386.3 11.7 %cholesky.16 = f32[128,128]{1,0:T(8,128)S(1)} custom-call(f32[128,128]{1,0:T(8,128)S(1)} %fusion.25), custom_call_target="Cholesky" | custom-call | tf_op jit(solution)/shard_map/jit(cholesky)/cholesky | solution.py:55
  398.1 0.6 compare_reduce_fusion
  398.7 0.7 fusion.21
  399.4 9.8 %custom-call.7 = f32[1,128,128]{1,2,0:T(8,128)S(1)} custom-call(f32[1,128,128]{2,1,0:T(8,128)S(1)} %fusion.21), custom_call_target="InvertDiagBlocksLowerTriangular" | custom-call | tf_op jit(solution)/shard_map/jit(_solve_triangular)/triangular_solve | solution.py:56
  409.2 0.2 fusion.23
  409.4 1.1 convolution_select_fusion
  410.5 0.0 all-gather.15.cloned.1.call-update
  410.5 0.0 all-gather.13.cloned.1.call-start
  410.6 15.6 %all-gather.15.cloned.1.call-done = f32[16,128,128]{2,1,0:T(8,128)} async-done(((f32[4,128,128]{2,1,0:T(8,128)}), f32[16,128,128]{2,1,0:T(8,128)}) %all-gather.15.cloned.1.call-update) | async-done | bytes 1048592 | tf_op jit(solution)/shard_map/all_gather | solution.py:15
  426.2 2.0 reduce_sum.28
  428.3 0.0 all-gather.13.cloned.1.call-update
  428.3 0.0 copy-done.3
  428.3 30.8 %all_gather.33 = f32[8,8,128]{2,1,0:T(8,128)S(1)} all-gather(f32[1,8,128]{2,1,0:T(8,128)S(1)} %slice_select_fusion.1), channel_id=1, replica_groups=mesh['rows'=8,'cols'=4] {'rows'}, dimensions={0}, use_global_device_ids=true | all-gather | bytes 36864 | tf_op jit(solution)/shard_map/all_gather | solution.py:15
  459.1 0.1 broadcast_and_fusion
  459.2 0.2 fusion.30
  459.4 1.9 fusion.14
  461.3 16.7 %all-gather.13.cloned.1.call-done = f32[4,1024,128]{2,1,0:T(8,128)} async-done(((f32[4,128,128]{2,1,0:T(8,128)}), f32[4,1024,128]{2,1,0:T(8,128)}) %all-gather.13.cloned.1.call-update) | async-done | bytes 2097168 | tf_op jit(solution)/shard_map/all_gather | solution.py:61
  478.0 4.3 select_subtract_fusion
  (12 shorter events, 0.1 us)
Async XLA Ops:
  7.2 39.7 %all-gather.7.cloned.1.call-start = ((), (), s32[]{:S(2)}) async-start(), calls=%async_computation | async-start | bytes 3932160 | tf_op jit(solution)/shard_map/all_gather | solution.py:33
  7.9 3.3 copy-start.2
  10.4 29.1 %copy-start.1 = (f32[4,128,4,256]{3,2,1,0:T(4,128)S(1)}, f32[4,128,4,256]{3,2,1,0:T(4,128)}, u32[]{:S(2)}) copy-start(f32[4,128,4,256]{3,2,1,0:T(4,128)} %param.7) | copy-start | bytes 6291460
  10.4 260.9 %all-gather.9.cloned.1.call-start = ((), (), s32[]{:S(2)}) async-start(), calls=%async_computation.1 | async-start | bytes 18874368 | tf_op jit(solution)/shard_map/all_gather | solution.py:38
  11.1 373.3 %all-gather.11.cloned.1.call-start = ((), (), s32[]{:S(2)}) async-start(), calls=%async_computation.2 | async-start | bytes 2162688 | tf_op jit(solution)/shard_map/all_gather | solution.py:15
  271.3 12.1 %copy-start = (f32[12,256,4,128]{3,1,0,2:T(8,128)S(1)}, f32[12,256,4,128]{3,1,0,2:T(8,128)}, u32[]{:S(2)}) copy-start(f32[12,256,4,128]{3,1,0,2:T(8,128)} %fusion.4) | copy-start | bytes 18874372
  271.3 12.1 %copy-start.4 = (f32[4,128]{1,0:T(4,128)S(1)}, f32[4,128]{1,0:T(4,128)}, u32[]{:S(2)}) copy-start(f32[4,128]{1,0:T(4,128)} %param.12) | copy-start | bytes 6148
  330.0 96.3 %all-gather.15.cloned.1.call-start = ((), (), s32[]{:S(2)}) async-start(), calls=%async_computation.4 | async-start | bytes 1310720 | tf_op jit(solution)/shard_map/all_gather | solution.py:15
  330.2 98.0 %copy-start.3 = (f32[4,8,128]{2,1,0:T(8,128)S(1)}, f32[4,8,128]{2,1,0:T(8,128)}, u32[]{:S(2)}) copy-start(f32[4,8,128]{2,1,0:T(8,128)} %param.13) | copy-start | bytes 49156
  410.5 67.5 %all-gather.13.cloned.1.call-start = ((), (), s32[]{:S(2)}) async-start(), calls=%async_computation.3 | async-start | bytes 2359296 | tf_op jit(solution)/shard_map/all_gather | solution.py:61
Sparse Core Ops, SparseCore 0:
  10.5 31.2 all-gather.6
  44.0 227.2 all-gather.8
  330.1 54.3 all-gather.10
  410.7 15.5 all-gather.14
  428.9 49.1 all-gather.12
